TPU v7x, 256 devices: a whole 4x4x8 slice. The times are simulated.
256 devices in a mesh: dp: 16 (over y, x_lo, core), cells: 16 (over z, x_hi).
Axes of the slice: x: 4 (x_hi: 2, x_lo: 2; x = x_hi * 2 + x_lo), y: 4, z: 8, core: 2. Of those that a mesh axis runs over, the one named last changes fastest.
Arguments:
- source_field: bfloat16 [48, 8, 12288], P(None, None, 'cells'), may hold values from -85 to 85, as said below
- receiver_field: bfloat16 [512, 8, 12288], P('dp', None, 'cells'), may hold values from -6 to 6
- source_index: int32 [8192], P('dp'), may hold values from 0 to 47
- receiver_index: int32 [8192], P('dp'), may hold values from 0 to 511, as said below
- observed: float32 [8192], P('dp'), may hold values from -6 to 6
- noise_code: int32 [8, 8192], P(None, 'dp'), may hold values from -4096 to 4096
- huber_code: int32 [8], replicated, may hold values from 8 to 40
- start_model: float32 [12288], P('cells'), may hold values from -6 to 6
Outputs:
- models: float32 [8, 12288], P(None, 'cells')
Inputs may be any that keep to these rules, and one draw needn't show every extreme that they name: `source_field`: entries of order one to ten; the scale varies from cell to cell. `receiver_index`: in each aligned block of 512 data, exactly 512 // 16 data name a receiver in each range [j * 32, (j + 1) * 32).
All inputs are finite; a program needn't handle non-finite values.
Results may differ from a plain program's by a relative error of at most 0.0011.
Values may be sent and summed in bfloat16 or wider, within the bound.
A program may use at most 64 MiB of HBM per device.

v0:
```python
import math
import jax
import jax.numpy as jnp
from jax import lax
from jax.sharding import PartitionSpec as P

ITERS = 2


def on_device(
    source_field,
    receiver_field,
    source_index,
    receiver_index,
    observed,
    noise_code,
    huber_code,
    start_model,
):
    count = huber_code.shape[0]
    thresh = (huber_code.astype(jnp.float32) / 16.0)[:, None]
    shifted = observed[None, :] + noise_code.astype(jnp.float32) / 4096.0
    receivers = lax.all_gather(receiver_field, "dp", axis=0, tiled=True)
    cells_local = source_field.shape[2]
    cells_total = cells_local * lax.axis_size("cells")
    components = source_field.shape[1]
    total = jnp.zeros((source_index.shape[0], cells_local), jnp.float32)
    for component in range(components):
        factor = 1.0 if component % 2 == 0 else -1.0
        source_part = source_field[source_index, component, :].astype(jnp.float32)
        receiver_part = receivers[receiver_index, component, :].astype(jnp.float32)
        total = total + factor * (source_part * receiver_part)
    kernel = (total * (0.2 / math.sqrt(components * cells_total))).astype(jnp.bfloat16)
    models = jnp.broadcast_to(start_model[None, :], (count, cells_local))
    velocity = jnp.zeros((count, cells_local), jnp.float32)
    for iteration in range(ITERS):
        model_half = models.astype(jnp.bfloat16)
        partial_sum = lax.dot_general(
            model_half, kernel, (((1,), (1,)), ((), ())), preferred_element_type=jnp.float32
        )
        predicted = lax.psum(partial_sum, "cells")
        weighted = jnp.clip(predicted - shifted, -thresh, thresh).astype(jnp.bfloat16)
        gradient_part = jnp.dot(weighted, kernel, preferred_element_type=jnp.float32)
        gradient = lax.psum(gradient_part, "dp")
        squares = lax.psum(jnp.sum(gradient * gradient, axis=1), "cells")
        scale_now = jnp.sqrt(squares / cells_total + 1e-06)[:, None]
        velocity = 0.9 * velocity + gradient / scale_now
        models = models - 0.1 * velocity
    return models


def solution(mesh):
    placed = (
        P(None, None, "cells"),
        P("dp", None, "cells"),
        P("dp"),
        P("dp"),
        P("dp"),
        P(None, "dp"),
        P(),
        P("cells"),
    )
    return jax.shard_map(
        on_device, mesh=mesh, in_specs=placed, out_specs=P(None, "cells"), check_vma=False
    )
```

profile of v0, /device:TPU:4, one launch (start us, length us, event | category | flops | bytes accessed | tf_op | source)
XLA Modules:
  0.0 487.7 jit_solution(16038923808687295108)
XLA Ops:
  6.5 0.7 all-gather.2.cloned.1.call-update
  7.3 0.7 fusion.17
  8.0 4.6 gather_fusion
  12.5 4.6 gather_fusion.10
  17.1 7.2 %gather_fusion.12 = bf16[512,768]{1,0:T(8,128)(2,1)} fusion(bf16[48,8,768]{2,1,0:T(8,128)(2,1)S(1)} %copy-done, s32[512]{0:T(512)S(1)} %get-tuple-element.12), kind=kCustom, calls=%fused_computation.12 | custom fusion | bytes 1576960 | tf_op jit(solution)/shard_map/gather | solution.py:30
  24.3 7.1 %gather_fusion.14 = bf16[512,768]{1,0:T(8,128)(2,1)} fusion(bf16[48,8,768]{2,1,0:T(8,128)(2,1)S(1)} %copy-done, s32[512]{0:T(512)S(1)} %get-tuple-element.6), kind=kCustom, calls=%fused_computation.14 | custom fusion | bytes 1576960 | tf_op jit(solution)/shard_map/gather | solution.py:30
  31.4 7.1 %gather_fusion.2 = bf16[512,768]{1,0:T(8,128)(2,1)} fusion(bf16[48,8,768]{2,1,0:T(8,128)(2,1)S(1)} %copy-done, s32[512]{0:T(512)S(1)} %get-tuple-element.7), kind=kCustom, calls=%fused_computation.2 | custom fusion | bytes 1576960 | tf_op jit(solution)/shard_map/gather | solution.py:30
  38.5 7.1 %gather_fusion.4 = bf16[512,768]{1,0:T(8,128)(2,1)} fusion(bf16[48,8,768]{2,1,0:T(8,128)(2,1)S(1)} %copy-done, s32[512]{0:T(512)S(1)} %get-tuple-element.8), kind=kCustom, calls=%fused_computation.4 | custom fusion | bytes 1576960 | tf_op jit(solution)/shard_map/gather | solution.py:30
  45.6 7.2 %gather_fusion.6 = bf16[512,768]{1,0:T(8,128)(2,1)} fusion(bf16[48,8,768]{2,1,0:T(8,128)(2,1)S(1)} %copy-done, s32[512]{0:T(512)S(1)} %get-tuple-element.9), kind=kCustom, calls=%fused_computation.6 | custom fusion | bytes 1576960 | tf_op jit(solution)/shard_map/gather | solution.py:30
  52.8 7.1 %gather_fusion.8 = bf16[512,768]{1,0:T(8,128)(2,1)} fusion(bf16[48,8,768]{2,1,0:T(8,128)(2,1)S(1)} %copy-done, s32[512]{0:T(512)S(1)} %get-tuple-element.10), kind=kCustom, calls=%fused_computation.8 | custom fusion | bytes 1576960 | tf_op jit(solution)/shard_map/gather | solution.py:30
  60.0 9.7 %gather_fusion.1 = bf16[512,768]{1,0:T(8,128)(2,1)} fusion(bf16[512,8,768]{2,1,0:T(8,128)(2,1)} %all-gather.2.cloned.1.call-done, s32[512]{0:T(512)S(1)} %get-tuple-element.13), kind=kCustom, calls=%fused_computation.1 | custom fusion | bytes 1576960 | tf_op jit(solution)/shard_map/gather | solution.py:31
  69.7 9.7 %gather_fusion.11 = bf16[512,768]{1,0:T(8,128)(2,1)} fusion(bf16[512,8,768]{2,1,0:T(8,128)(2,1)} %all-gather.2.cloned.1.call-done, s32[512]{0:T(512)S(1)} %get-tuple-element.19), kind=kCustom, calls=%fused_computation.11 | custom fusion | bytes 1576960 | tf_op jit(solution)/shard_map/gather | solution.py:31
  79.4 9.8 %gather_fusion.13 = bf16[512,768]{1,0:T(8,128)(2,1)} fusion(bf16[512,8,768]{2,1,0:T(8,128)(2,1)} %all-gather.2.cloned.1.call-done, s32[512]{0:T(512)S(1)} %get-tuple-element.20), kind=kCustom, calls=%fused_computation.13 | custom fusion | bytes 1576960 | tf_op jit(solution)/shard_map/gather | solution.py:31
  89.2 9.7 %gather_fusion.15 = bf16[512,768]{1,0:T(8,128)(2,1)} fusion(bf16[512,8,768]{2,1,0:T(8,128)(2,1)} %all-gather.2.cloned.1.call-done, s32[512]{0:T(512)S(1)} %get-tuple-element.14), kind=kCustom, calls=%fused_computation.15 | custom fusion | bytes 1576960 | tf_op jit(solution)/shard_map/gather | solution.py:31
  98.9 9.7 %gather_fusion.3 = bf16[512,768]{1,0:T(8,128)(2,1)} fusion(bf16[512,8,768]{2,1,0:T(8,128)(2,1)} %all-gather.2.cloned.1.call-done, s32[512]{0:T(512)S(1)} %get-tuple-element.15), kind=kCustom, calls=%fused_computation.3 | custom fusion | bytes 1576960 | tf_op jit(solution)/shard_map/gather | solution.py:31
  108.6 9.7 %gather_fusion.5 = bf16[512,768]{1,0:T(8,128)(2,1)} fusion(bf16[512,8,768]{2,1,0:T(8,128)(2,1)} %all-gather.2.cloned.1.call-done, s32[512]{0:T(512)S(1)} %get-tuple-element.16), kind=kCustom, calls=%fused_computation.5 | custom fusion | bytes 1576960 | tf_op jit(solution)/shard_map/gather | solution.py:31
  118.3 9.7 %gather_fusion.7 = bf16[512,768]{1,0:T(8,128)(2,1)} fusion(bf16[512,8,768]{2,1,0:T(8,128)(2,1)} %all-gather.2.cloned.1.call-done, s32[512]{0:T(512)S(1)} %get-tuple-element.17), kind=kCustom, calls=%fused_computation.7 | custom fusion | bytes 1576960 | tf_op jit(solution)/shard_map/gather | solution.py:31
  128.0 9.7 %gather_fusion.9 = bf16[512,768]{1,0:T(8,128)(2,1)} fusion(bf16[512,8,768]{2,1,0:T(8,128)(2,1)} %all-gather.2.cloned.1.call-done, s32[512]{0:T(512)S(1)} %get-tuple-element.18), kind=kCustom, calls=%fused_computation.9 | custom fusion | bytes 1576960 | tf_op jit(solution)/shard_map/gather | solution.py:31
  137.8 6.0 %multiply_convert_fusion = bf16[512,768]{1,0:T(8,128)(2,1)S(1)} fusion(bf16[512,768]{1,0:T(8,128)(2,1)} %gather_fusion.15, bf16[512,768]{1,0:T(8,128)(2,1)} %gather_fusion.14, bf16[512,768]{1,0:T(8,128)(2,1)} %gather_fusion.13, bf16[512,768]{1,0:T(8,128)(2,1)} %gather_fusion.12, bf16[512,768]{1,0:T(8,128)(2,1)} %gather_fusion.11, ...), kind=kLoop, calls=%fused_computation.16 | loop fusion | flops 14548992 | bytes 13369344 | tf_op jit(solution)/shard_map/convert_element_type | solution.py:33
  143.8 0.3 convolution_bitcast_fusion
  144.1 74.7 %psum.42 = f32[8,512]{1,0:T(8,128)S(1)} all-reduce(f32[8,512]{1,0:T(8,128)S(1)} %convolution_bitcast_fusion), channel_id=1, replica_groups=mesh['dp'=16,'cells'=16] {'cells'}, use_global_device_ids=true, to_apply=%region_0.0 | all-reduce | flops 4096 | bytes 32768 | tf_op jit(solution)/shard_map/psum | solution.py:41
  218.8 0.2 fusion.5
  219.1 52.9 %psum.43 = f32[8,768]{1,0:T(8,128)S(1)} all-reduce(f32[8,768]{1,0:T(8,128)S(1)} %fusion.5), channel_id=1, replica_groups=mesh['dp'=16,'cells'=16] {'dp'}, use_global_device_ids=true, to_apply=%region_1.2 | all-reduce | flops 6144 | bytes 49152 | tf_op jit(solution)/shard_map/psum | solution.py:44
  272.0 0.1 multiply_reduce_fusion.1
  272.1 42.5 %psum.44 = f32[8]{0:T(128)S(1)} all-reduce(f32[8]{0:T(128)S(1)} %multiply_reduce_fusion.1), channel_id=1, replica_groups=mesh['dp'=16,'cells'=16] {'cells'}, use_global_device_ids=true, to_apply=%region_3.4 | all-reduce | flops 8 | bytes 64 | tf_op jit(solution)/shard_map/psum | solution.py:45
  314.6 0.3 fusion.1
  314.9 69.7 %psum.45 = f32[8,512]{1,0:T(8,128)S(1)} all-reduce(f32[8,512]{1,0:T(8,128)S(1)} %fusion.1), channel_id=1, replica_groups=mesh['dp'=16,'cells'=16] {'cells'}, use_global_device_ids=true, to_apply=%region_4.5 | all-reduce | flops 4096 | bytes 32768 | tf_op jit(solution)/shard_map/psum | solution.py:41
  384.6 0.2 fusion.6
  384.9 52.9 %psum.46 = f32[8,768]{1,0:T(8,128)S(1)} all-reduce(f32[8,768]{1,0:T(8,128)S(1)} %fusion.6), channel_id=1, replica_groups=mesh['dp'=16,'cells'=16] {'dp'}, use_global_device_ids=true, to_apply=%region_5.6 | all-reduce | flops 6144 | bytes 49152 | tf_op jit(solution)/shard_map/psum | solution.py:44
  437.8 0.1 multiply_reduce_fusion
  437.9 42.2 %psum.47 = f32[8]{0:T(128)S(1)} all-reduce(f32[8]{0:T(128)S(1)} %multiply_reduce_fusion), channel_id=1, replica_groups=mesh['dp'=16,'cells'=16] {'cells'}, use_global_device_ids=true, to_apply=%region_7.8 | all-reduce | flops 8 | bytes 64 | tf_op jit(solution)/shard_map/psum | solution.py:45
  480.1 0.7 multiply_subtract_fusion
  (19 shorter events, 0.1 us)
Async XLA Ops:
  6.5 1.4 copy-start
  6.5 53.4 %all-gather.2.cloned.1.call-start = ((), (), s32[]{:S(2)}) async-start(), calls=%async_computation | async-start | bytes 6684672 | tf_op jit(solution)/shard_map/all_gather | solution.py:23
  52.8 7.1 %copy-start.2 = (f32[768]{0:T(1024)S(1)}, f32[768]{0:T(1024)}, u32[]{:S(2)}) copy-start(f32[768]{0:T(1024)} %param.15) | copy-start | bytes 9220
  52.8 7.1 %copy-start.5 = (s32[8]{0:T(128)S(1)}, s32[8]{0:T(128)}, u32[]{:S(2)}) copy-start(s32[8]{0:T(128)} %param.14) | copy-start | bytes 100
  52.8 7.2 %copy-start.4 = (s32[512]{0:T(512)S(1)}, s32[512]{0:T(512)}, u32[]{:S(2)}) copy-start(s32[512]{0:T(512)} %param.11) | copy-start | bytes 6148
  137.8 81.0 %copy-start.1 = (s32[8,512]{1,0:T(8,128)S(1)}, s32[8,512]{1,0:T(8,128)}, u32[]{:S(2)}) copy-start(s32[8,512]{1,0:T(8,128)} %param.13) | copy-start | bytes 49156
  137.8 81.0 %copy-start.3 = (f32[512]{0:T(512)S(1)}, f32[512]{0:T(512)}, u32[]{:S(2)}) copy-start(f32[512]{0:T(512)} %param.12) | copy-start | bytes 6148
Sparse Core Ops, SparseCore 0:
  9.2 47.6 all-gather.1
where the time goes:
time: 489 us; the launch traced here: 488 us
  blocking collectives  335 us (69%)
  local copies, waits for them, and re-layouts  130 us (27%)
  between operations  13.5 us (3%)
  other arithmetic  7.68 us (2%)
    psum x2, blocking collectives, on_device(): predicted = lax.psum(partial_sum, 'cells')  144 us
    psum x2, blocking collectives, on_device(): gradient = lax.psum(gradient_part, 'dp')  106 us
    psum x2, blocking collectives, on_device(): squares = lax.psum(jnp.sum(gradient * gradient, axis=1), 'cells')  84.7 us
    gather x8, local copies, waits for them, and re-layouts, on_device(): receiver_part = receivers[receiver_index, component, :].astype(jnp.float32)  77.8 us
    gather x8, local copies, waits for them, and re-layouts, on_device(): source_part = source_field[source_index, component, :].astype(jnp.float32)  51.9 us
  transfers between devices with their start and end apart: 1, of which 0 were waited for; matrix products, arithmetic and copies ran while one was open for 11% of the time, Pallas kernels for 0%

commit v1 on v0

--- a/solution.py
+++ b/solution.py
@@ -38,7 +38,8 @@
         partial_sum = lax.dot_general(
             model_half, kernel, (((1,), (1,)), ((), ())), preferred_element_type=jnp.float32
         )
-        predicted = lax.psum(partial_sum, "cells")
+        parts = lax.all_gather(partial_sum, "cells")
+        predicted = jnp.sum(parts, axis=0)
         weighted = jnp.clip(predicted - shifted, -thresh, thresh).astype(jnp.bfloat16)
         gradient_part = jnp.dot(weighted, kernel, preferred_element_type=jnp.float32)
         gradient = lax.psum(gradient_part, "dp")

time: 489 us -> 419 us (0.86)
  blocking collectives: 335 us -> 265 us
    psum x2 -> x0, blocking collectives: 144 us -> none  [on_device(): predicted = lax.psum(partial_sum, 'cells')]
    all_gather x0 -> x2, blocking collectives: none -> 77.6 us  [on_device(): parts = lax.all_gather(partial_sum, 'cells')]
  transfers between devices with their start and end apart: 1 -> 1, of which waited for: 0 -> 0; matrix products, arithmetic and copies ran while one was open for 11% -> 13% of each run, Pallas kernels for 0% -> 0%
where the time goes in v1:
time: 419 us; the launch traced here: 418 us
  blocking collectives  265 us (63%)
  local copies, waits for them, and re-layouts  130 us (31%)
  between operations  13.5 us (3%)
  other arithmetic  7.72 us (2%)
    psum x2, blocking collectives, on_device(): gradient = lax.psum(gradient_part, 'dp')  107 us
    psum x2, blocking collectives, on_device(): squares = lax.psum(jnp.sum(gradient * gradient, axis=1), 'cells')  80.9 us
    gather x8, local copies, waits for them, and re-layouts, on_device(): receiver_part = receivers[receiver_index, component, :].astype(jnp.float32)  77.8 us
    all_gather x2, blocking collectives, on_device(): parts = lax.all_gather(partial_sum, 'cells')  77.6 us
    gather x8, local copies, waits for them, and re-layouts, on_device(): source_part = source_field[source_index, component, :].astype(jnp.float32)  51.9 us
  transfers between devices with their start and end apart: 1, of which 0 were waited for; matrix products, arithmetic and copies ran while one was open for 13% of the time, Pallas kernels for 0%

profile of v1, /device:TPU:4, one launch (start us, length us, event | category | flops | bytes accessed | tf_op | source)
XLA Modules:
  0.0 418.0 jit_solution(6154154334488081067)
XLA Ops:
  6.5 0.7 all-gather.4.cloned.1.call-update
  7.3 0.7 fusion.17
  8.0 4.6 %gather_fusion = bf16[512,768]{1,0:T(8,128)(2,1)S(1)} fusion(bf16[48,8,768]{2,1,0:T(8,128)(2,1)S(1)} %copy-done, s32[512]{0:T(512)S(1)} %get-tuple-element.5), kind=kCustom, calls=%fused_computation | custom fusion | bytes 1576960 | tf_op jit(solution)/shard_map/gather | solution.py:30
  12.5 4.6 %gather_fusion.10 = bf16[512,768]{1,0:T(8,128)(2,1)S(1)} fusion(bf16[48,8,768]{2,1,0:T(8,128)(2,1)S(1)} %copy-done, s32[512]{0:T(512)S(1)} %get-tuple-element.11), kind=kCustom, calls=%fused_computation.10 | custom fusion | bytes 1576960 | tf_op jit(solution)/shard_map/gather | solution.py:30
  17.1 7.2 %gather_fusion.12 = bf16[512,768]{1,0:T(8,128)(2,1)} fusion(bf16[48,8,768]{2,1,0:T(8,128)(2,1)S(1)} %copy-done, s32[512]{0:T(512)S(1)} %get-tuple-element.12), kind=kCustom, calls=%fused_computation.12 | custom fusion | bytes 1576960 | tf_op jit(solution)/shard_map/gather | solution.py:30
  24.3 7.1 %gather_fusion.14 = bf16[512,768]{1,0:T(8,128)(2,1)} fusion(bf16[48,8,768]{2,1,0:T(8,128)(2,1)S(1)} %copy-done, s32[512]{0:T(512)S(1)} %get-tuple-element.6), kind=kCustom, calls=%fused_computation.14 | custom fusion | bytes 1576960 | tf_op jit(solution)/shard_map/gather | solution.py:30
  31.4 7.1 %gather_fusion.2 = bf16[512,768]{1,0:T(8,128)(2,1)} fusion(bf16[48,8,768]{2,1,0:T(8,128)(2,1)S(1)} %copy-done, s32[512]{0:T(512)S(1)} %get-tuple-element.7), kind=kCustom, calls=%fused_computation.2 | custom fusion | bytes 1576960 | tf_op jit(solution)/shard_map/gather | solution.py:30
  38.5 7.1 %gather_fusion.4 = bf16[512,768]{1,0:T(8,128)(2,1)} fusion(bf16[48,8,768]{2,1,0:T(8,128)(2,1)S(1)} %copy-done, s32[512]{0:T(512)S(1)} %get-tuple-element.8), kind=kCustom, calls=%fused_computation.4 | custom fusion | bytes 1576960 | tf_op jit(solution)/shard_map/gather | solution.py:30
  45.6 7.2 %gather_fusion.6 = bf16[512,768]{1,0:T(8,128)(2,1)} fusion(bf16[48,8,768]{2,1,0:T(8,128)(2,1)S(1)} %copy-done, s32[512]{0:T(512)S(1)} %get-tuple-element.9), kind=kCustom, calls=%fused_computation.6 | custom fusion | bytes 1576960 | tf_op jit(solution)/shard_map/gather | solution.py:30
  52.8 7.1 %gather_fusion.8 = bf16[512,768]{1,0:T(8,128)(2,1)} fusion(bf16[48,8,768]{2,1,0:T(8,128)(2,1)S(1)} %copy-done, s32[512]{0:T(512)S(1)} %get-tuple-element.10), kind=kCustom, calls=%fused_computation.8 | custom fusion | bytes 1576960 | tf_op jit(solution)/shard_map/gather | solution.py:30
  60.0 9.7 %gather_fusion.1 = bf16[512,768]{1,0:T(8,128)(2,1)} fusion(bf16[512,8,768]{2,1,0:T(8,128)(2,1)} %all-gather.4.cloned.1.call-done, s32[512]{0:T(512)S(1)} %get-tuple-element.13), kind=kCustom, calls=%fused_computation.1 | custom fusion | bytes 1576960 | tf_op jit(solution)/shard_map/gather | solution.py:31
  69.7 9.7 %gather_fusion.11 = bf16[512,768]{1,0:T(8,128)(2,1)} fusion(bf16[512,8,768]{2,1,0:T(8,128)(2,1)} %all-gather.4.cloned.1.call-done, s32[512]{0:T(512)S(1)} %get-tuple-element.19), kind=kCustom, calls=%fused_computation.11 | custom fusion | bytes 1576960 | tf_op jit(solution)/shard_map/gather | solution.py:31
  79.4 9.8 %gather_fusion.13 = bf16[512,768]{1,0:T(8,128)(2,1)} fusion(bf16[512,8,768]{2,1,0:T(8,128)(2,1)} %all-gather.4.cloned.1.call-done, s32[512]{0:T(512)S(1)} %get-tuple-element.20), kind=kCustom, calls=%fused_computation.13 | custom fusion | bytes 1576960 | tf_op jit(solution)/shard_map/gather | solution.py:31
  89.2 9.7 %gather_fusion.15 = bf16[512,768]{1,0:T(8,128)(2,1)} fusion(bf16[512,8,768]{2,1,0:T(8,128)(2,1)} %all-gather.4.cloned.1.call-done, s32[512]{0:T(512)S(1)} %get-tuple-element.14), kind=kCustom, calls=%fused_computation.15 | custom fusion | bytes 1576960 | tf_op jit(solution)/shard_map/gather | solution.py:31
  98.9 9.7 %gather_fusion.3 = bf16[512,768]{1,0:T(8,128)(2,1)} fusion(bf16[512,8,768]{2,1,0:T(8,128)(2,1)} %all-gather.4.cloned.1.call-done, s32[512]{0:T(512)S(1)} %get-tuple-element.15), kind=kCustom, calls=%fused_computation.3 | custom fusion | bytes 1576960 | tf_op jit(solution)/shard_map/gather | solution.py:31
  108.6 9.7 %gather_fusion.5 = bf16[512,768]{1,0:T(8,128)(2,1)} fusion(bf16[512,8,768]{2,1,0:T(8,128)(2,1)} %all-gather.4.cloned.1.call-done, s32[512]{0:T(512)S(1)} %get-tuple-element.16), kind=kCustom, calls=%fused_computation.5 | custom fusion | bytes 1576960 | tf_op jit(solution)/shard_map/gather | solution.py:31
  118.3 9.7 %gather_fusion.7 = bf16[512,768]{1,0:T(8,128)(2,1)} fusion(bf16[512,8,768]{2,1,0:T(8,128)(2,1)} %all-gather.4.cloned.1.call-done, s32[512]{0:T(512)S(1)} %get-tuple-element.17), kind=kCustom, calls=%fused_computation.7 | custom fusion | bytes 1576960 | tf_op jit(solution)/shard_map/gather | solution.py:31
  128.0 9.7 %gather_fusion.9 = bf16[512,768]{1,0:T(8,128)(2,1)} fusion(bf16[512,8,768]{2,1,0:T(8,128)(2,1)} %all-gather.4.cloned.1.call-done, s32[512]{0:T(512)S(1)} %get-tuple-element.18), kind=kCustom, calls=%fused_computation.9 | custom fusion | bytes 1576960 | tf_op jit(solution)/shard_map/gather | solution.py:31
  137.8 6.0 %multiply_convert_fusion = bf16[512,768]{1,0:T(8,128)(2,1)S(1)} fusion(bf16[512,768]{1,0:T(8,128)(2,1)} %gather_fusion.15, bf16[512,768]{1,0:T(8,128)(2,1)} %gather_fusion.14, bf16[512,768]{1,0:T(8,128)(2,1)} %gather_fusion.13, bf16[512,768]{1,0:T(8,128)(2,1)} %gather_fusion.12, bf16[512,768]{1,0:T(8,128)(2,1)} %gather_fusion.11, ...), kind=kLoop, calls=%fused_computation.16 | loop fusion | flops 14548992 | bytes 13369344 | tf_op jit(solution)/shard_map/convert_element_type | solution.py:33
  143.8 0.3 convolution_bitcast_fusion
  144.1 40.6 %all-gather = f32[128,512]{1,0:T(8,128)S(1)} all-gather(f32[8,512]{1,0:T(8,128)S(1)} %convolution_bitcast_fusion), channel_id=2, replica_groups=mesh['dp'=16,'cells'=16] {'cells'}, dimensions={0}, use_global_device_ids=true | all-gather | bytes 278528 | tf_op jit(solution)/shard_map/all_gather | solution.py:41
  184.7 0.2 fusion.5
  185.0 53.8 %psum.28 = f32[8,768]{1,0:T(8,128)S(1)} all-reduce(f32[8,768]{1,0:T(8,128)S(1)} %fusion.5), channel_id=1, replica_groups=mesh['dp'=16,'cells'=16] {'dp'}, use_global_device_ids=true, to_apply=%region_1.2 | all-reduce | flops 6144 | bytes 49152 | tf_op jit(solution)/shard_map/psum | solution.py:45
  238.8 0.1 multiply_reduce_fusion.1
  238.9 40.9 %psum.29 = f32[8]{0:T(128)S(1)} all-reduce(f32[8]{0:T(128)S(1)} %multiply_reduce_fusion.1), channel_id=1, replica_groups=mesh['dp'=16,'cells'=16] {'cells'}, use_global_device_ids=true, to_apply=%region_3.4 | all-reduce | flops 8 | bytes 64 | tf_op jit(solution)/shard_map/psum | solution.py:46
  279.8 0.3 fusion.1
  280.1 37.0 %all-gather.1 = f32[128,512]{1,0:T(8,128)S(1)} all-gather(f32[8,512]{1,0:T(8,128)S(1)} %fusion.1), channel_id=3, replica_groups=mesh['dp'=16,'cells'=16] {'cells'}, dimensions={0}, use_global_device_ids=true | all-gather | bytes 278528 | tf_op jit(solution)/shard_map/all_gather | solution.py:41
  317.2 0.2 fusion.6
  317.4 52.9 %psum.30 = f32[8,768]{1,0:T(8,128)S(1)} all-reduce(f32[8,768]{1,0:T(8,128)S(1)} %fusion.6), channel_id=1, replica_groups=mesh['dp'=16,'cells'=16] {'dp'}, use_global_device_ids=true, to_apply=%region_5.6 | all-reduce | flops 6144 | bytes 49152 | tf_op jit(solution)/shard_map/psum | solution.py:45
  370.3 0.1 multiply_reduce_fusion
  370.4 40.0 %psum.31 = f32[8]{0:T(128)S(1)} all-reduce(f32[8]{0:T(128)S(1)} %multiply_reduce_fusion), channel_id=1, replica_groups=mesh['dp'=16,'cells'=16] {'cells'}, use_global_device_ids=true, to_apply=%region_7.8 | all-reduce | flops 8 | bytes 64 | tf_op jit(solution)/shard_map/psum | solution.py:46
  410.5 0.7 multiply_subtract_fusion
  (21 shorter events, 0.1 us)
Async XLA Ops:
  6.5 1.4 copy-start
  6.5 53.4 %all-gather.4.cloned.1.call-start = ((), (), s32[]{:S(2)}) async-start(), calls=%async_computation | async-start | bytes 6684672 | tf_op jit(solution)/shard_map/all_gather | solution.py:23
  52.8 7.1 %copy-start.2 = (f32[768]{0:T(1024)S(1)}, f32[768]{0:T(1024)}, u32[]{:S(2)}) copy-start(f32[768]{0:T(1024)} %param.15) | copy-start | bytes 9220
  52.8 7.1 %copy-start.5 = (s32[8]{0:T(128)S(1)}, s32[8]{0:T(128)}, u32[]{:S(2)}) copy-start(s32[8]{0:T(128)} %param.14) | copy-start | bytes 100
  52.8 7.2 %copy-start.4 = (s32[512]{0:T(512)S(1)}, s32[512]{0:T(512)}, u32[]{:S(2)}) copy-start(s32[512]{0:T(512)} %param.11) | copy-start | bytes 6148
  137.8 46.9 %copy-start.1 = (s32[8,512]{1,0:T(8,128)S(1)}, s32[8,512]{1,0:T(8,128)}, u32[]{:S(2)}) copy-start(s32[8,512]{1,0:T(8,128)} %param.13) | copy-start | bytes 49156
  137.8 47.0 %copy-start.3 = (f32[512]{0:T(512)S(1)}, f32[512]{0:T(512)}, u32[]{:S(2)}) copy-start(f32[512]{0:T(512)} %param.12) | copy-start | bytes 6148
Sparse Core Ops, SparseCore 0:
  9.2 47.6 all-gather.3
